TPU v7x, 256 devices: a whole 4x4x8 slice. The times are simulated.
256 devices in a mesh: node: 16 (over z, core), head: 16 (over x, y).
Axes of the slice: x: 4, y: 4, z: 8, core: 2. Of those that a mesh axis runs over, the one named last changes fastest.
Arguments:
- features: bfloat16 [65536, 1024], P(('node', 'head')), may hold values from -6 to 6
- attn_gain: float32 [1024], replicated, may hold values from 0.25 to 1.75
- qkv_weight: bfloat16 [1024, 16, 192], P(None, 'head')
- out_weight: bfloat16 [1024, 1024], replicated, may hold values from -0.1875 to 0.1875
- feedforward_norm_gain: float32 [1024], replicated, may hold values from 0.25 to 1.75
- up_weight: bfloat16 [1024, 2048], replicated, may hold values from -0.1875 to 0.1875
- down_weight: bfloat16 [2048, 1024], replicated, may hold values from -0.125 to 0.125
- tile_pattern: int32 [512, 8], P('node'), may hold values from 0 to 511, as said below
- node_order: int32 [16, 4096], P('node'), may hold values from 0 to 4095, each once within a row
Outputs:
- updated: bfloat16 [65536, 1024], P(('node', 'head'))
Inputs may be any that keep to these rules, and one draw needn't show every extreme that they name: `tile_pattern`: row t names 8 different tiles; the first is t itself; all lie in partitions (tiles p * 32 to (p + 1) * 32 - 1) at cyclic distance at most 2 from t's partition; the second lies 2 partitions below t's and the third 2 above. `node_order`: each row lists every local row of its partition once.
All inputs are finite; a program needn't handle non-finite values.
Results may differ from a plain program's by a relative error of at most 0.0045.
Values may be sent and summed in bfloat16 or wider, within the bound.
A program may use at most 64 MiB of HBM per device.

v0:
```python
import math
import jax
import jax.numpy as jnp
from jax import lax
from jax.sharding import PartitionSpec as P

D = 1024
HD = 64
TILE = 128
NNZ = 8
REACH = 2


def passed_along(x, axis, by):
    size = lax.axis_size(axis)
    return lax.ppermute(x, axis, [(i, (i + by) % size) for i in range(size)])


def layer_norm(values, gain):
    row_mean = jnp.mean(values, -1, keepdims=True)
    centred = values - row_mean
    variance = jnp.mean(centred * centred, -1, keepdims=True)
    return centred * lax.rsqrt(variance + 1e-05) * gain


def shards(
    features,
    attn_gain,
    qkv_weight,
    out_weight,
    feedforward_norm_gain,
    up_weight,
    down_weight,
    tile_pattern,
    node_order,
):
    own_rows = features.shape[0]
    local_heads = qkv_weight.shape[1]
    head_placements = lax.axis_size("head")
    partitions = lax.axis_size("node")
    rows_part = own_rows * head_placements
    query_tiles = rows_part // TILE
    normed = layer_norm(features.astype(jnp.float32), attn_gain).astype(jnp.bfloat16)
    reordered_weight = jnp.concatenate([qkv_weight[:, :, HD:], qkv_weight[:, :, :HD]], -1)
    local_weight = reordered_weight.reshape(D, local_heads * 3 * HD)
    projected = jnp.dot(
        lax.all_gather(normed, "head", axis=0, tiled=True),
        local_weight,
        preferred_element_type=jnp.float32,
    ).astype(jnp.bfloat16)
    projected = projected.reshape(rows_part, local_heads, 3 * HD)
    partition_permutation = node_order[0]
    keyval_rows = projected[:, :, : 2 * HD].reshape(rows_part, local_heads * 2 * HD)
    query_rows = projected[:, :, 2 * HD :].reshape(rows_part, local_heads * HD)
    keyval = jnp.take(keyval_rows, partition_permutation, axis=0)
    queries = jnp.take(query_rows, partition_permutation, axis=0)
    current = passed_along(keyval, "node", -REACH)
    blocks = [current]
    for cycle_step in range(2 * REACH):
        current = passed_along(current, "node", 1)
        blocks.append(current)
    window = jnp.stack(blocks[::-1])
    window_tiles = window.reshape((2 * REACH + 1) * query_tiles, TILE, local_heads * 2 * HD)
    partition = lax.axis_index("node")
    window_position = (
        tile_pattern // query_tiles - partition + REACH + partitions
    ) % partitions * query_tiles + tile_pattern % query_tiles
    tile_group = math.gcd(query_tiles, max(1, 512 // TILE))
    score_scale = 1.0 / math.sqrt(HD)

    def attend(item_pair):
        group_queries, columns = item_pair
        picked = jnp.take(window_tiles, columns.reshape(tile_group * NNZ), axis=0)
        picked = picked.reshape(tile_group, NNZ * TILE, local_heads, 2 * HD)
        key_rows = picked[..., :HD]
        value_rows = picked[..., HD:]
        query_block = group_queries.reshape(tile_group, TILE, local_heads, HD)
        scores = (
            jnp.einsum("gqhd,gmhd->ghqm", query_block, key_rows, preferred_element_type=jnp.float32)
            * score_scale
        )
        row_max = jnp.max(scores, -1, keepdims=True)
        expd = jnp.exp(scores - row_max)
        weight_arrays = (expd / jnp.sum(expd, -1, keepdims=True)).astype(jnp.bfloat16)
        result = jnp.einsum(
            "ghqm,gmhd->gqhd", weight_arrays, value_rows, preferred_element_type=jnp.float32
        ).astype(jnp.bfloat16)
        return result.reshape(tile_group * TILE, local_heads * HD)

    grouped_queries = queries.reshape(
        query_tiles // tile_group, tile_group * TILE, local_heads * HD
    )
    grouped_slots = window_position.reshape(query_tiles // tile_group, tile_group, NNZ)
    attended = lax.map(attend, (grouped_queries, grouped_slots)).reshape(
        rows_part, local_heads * HD
    )
    inverse_order = (
        jnp.zeros((rows_part,), jnp.int32)
        .at[partition_permutation]
        .set(jnp.arange(rows_part, dtype=jnp.int32))
    )
    restored = jnp.take(attended, inverse_order, axis=0)
    gathered_heads = lax.all_to_all(restored, "head", split_axis=0, concat_axis=1, tiled=True)
    residual = features.astype(jnp.float32) + jnp.dot(
        gathered_heads, out_weight, preferred_element_type=jnp.float32
    )
    mlp_input = layer_norm(residual, feedforward_norm_gain).astype(jnp.bfloat16)
    hidden = jax.nn.gelu(jnp.dot(mlp_input, up_weight, preferred_element_type=jnp.float32)).astype(
        jnp.bfloat16
    )
    return (residual + jnp.dot(hidden, down_weight, preferred_element_type=jnp.float32)).astype(
        jnp.bfloat16
    )


def solution(mesh):
    return jax.shard_map(
        shards,
        mesh=mesh,
        in_specs=(
            P(("node", "head"), None),
            P(),
            P(None, "head", None),
            P(),
            P(),
            P(),
            P(),
            P("node", None),
            P("node", None),
        ),
        out_specs=P(("node", "head"), None),
        check_vma=False,
    )
```

profile of v0, /device:TPU:96, one launch (start us, length us, event | category | flops | bytes accessed | tf_op | source)
XLA Modules:
  0.0 371.6 jit_solution(18285803736506806688)
XLA Ops:
  9.3 2.1 fusion.37
  11.5 77.8 %all-gather.2.cloned.1.call-done = bf16[4096,1024]{1,0:T(8,128)(2,1)} async-done(((bf16[256,1024]{1,0:T(8,128)(2,1)}), bf16[4096,1024]{1,0:T(8,128)(2,1)}) %all-gather.2.cloned.1.call-update) | async-done | bytes 8388624 | tf_op jit(solution)/shard_map/all_gather | solution.py:47
  89.3 6.3 %fusion.23 = bf16[4096,1,192]{0,2,1:T(8,128)(2,1)S(1)} fusion(bf16[4096,1024]{1,0:T(8,128)(2,1)} %all-gather.2.cloned.1.call-done, bf16[1024,1,64]{0,2,1:T(8,128)(2,1)S(1)} %slice-done, bf16[1024,1,128]{0,2,1:T(8,128)(2,1)S(1)} %slice-done.1), kind=kOutput, calls=%fused_computation.33 | convolution fusion | flops 1612185600 | bytes 10354688 | tf_op jit(solution)/shard_map/dot_general | solution.py:46
  97.8 1.6 copy.17
  99.4 15.0 %gather_fusion.1 = bf16[4096,128]{1,0:T(8,128)(2,1)} fusion(bf16[4096,128]{1,0:T(8,128)(2,1)S(1)} %copy.17, s32[4096]{0:T(1024)S(1)} %broadcast_clamp_fusion), kind=kCustom, calls=%fused_computation.3 | custom fusion | bytes 2113536 | tf_op jit(solution)/shard_map/jit(_take)/gather | solution.py:55
  114.4 3.4 broadcast_select_fusion.3
  118.3 25.5 %collective-permute-done = bf16[4096,128]{1,0:T(8,128)(2,1)S(1)} collective-permute-done((bf16[4096,128]{1,0:T(8,128)(2,1)S(1)}, bf16[4096,128]{1,0:T(8,128)(2,1)S(1)}, u32[]{:S(2)}, u32[]{:S(2)}) %collective-permute-start) | collective-permute-done | bytes 1048608 | tf_op jit(solution)/shard_map/ppermute | solution.py:16
  144.8 14.2 %collective-permute-done.1 = bf16[4096,128]{1,0:T(8,128)(2,1)S(1)} collective-permute-done((bf16[4096,128]{1,0:T(8,128)(2,1)S(1)}, bf16[4096,128]{1,0:T(8,128)(2,1)S(1)}, u32[]{:S(2)}, u32[]{:S(2)}) %collective-permute-start.1) | collective-permute-done | bytes 1048608 | tf_op jit(solution)/shard_map/ppermute | solution.py:16
  160.0 14.2 %collective-permute-done.2 = bf16[4096,128]{1,0:T(8,128)(2,1)S(1)} collective-permute-done((bf16[4096,128]{1,0:T(8,128)(2,1)S(1)}, bf16[4096,128]{1,0:T(8,128)(2,1)S(1)}, u32[]{:S(2)}, u32[]{:S(2)}) %collective-permute-start.2) | collective-permute-done | bytes 1048608 | tf_op jit(solution)/shard_map/ppermute | solution.py:16
  174.7 15.7 %scatter_custom_fusion = s32[4096]{0:T(1024)S(1)} fusion(s32[4096]{0:T(1024)S(1)} %bitcast.103, s32[4096]{0:T(1024)S(1)} %iota.3, s32[]{:T(128)} %copy.60), kind=kCustom, calls=%fused_computation.84 | custom fusion | bytes 16388 | tf_op jit(solution)/shard_map/scatter | solution.py:100
  190.5 3.7 collective-permute-start.4
  194.2 1.9 slice_bitcast_fusion.15
  196.1 1.5 copy.18
  197.6 15.0 %gather_fusion.2 = bf16[4096,64]{1,0:T(8,128)(2,1)} fusion(bf16[4096,64]{1,0:T(8,128)(2,1)S(1)} %copy.18, s32[4096]{0:T(1024)S(1)} %get-tuple-element.53), kind=kCustom, calls=%fused_computation.clone | custom fusion | bytes 1064960 | tf_op jit(solution)/shard_map/jit(_take)/gather | solution.py:56
  212.6 3.4 broadcast_select_fusion.2
  218.5 1.4 bitcast_dynamic-update-slice_fusion.3
  221.4 2.3 copy-done.3
  223.7 92.5 %while.10 = (s32[]{:T(128)}, bf16[8,512,64]{1,2,0:T(8,128)(2,1)}, s32[8,4,8]{2,1,0:T(4,128)S(1)}, bf16[160,128,128]{2,1,0:T(8,128)(2,1)}, bf16[8,512,64]{1,2,0:T(8,128)(2,1)}, /*index=5*/s32[]{:T(128)}) while((s32[]{:T(128)}, bf16[8,512,64]{1,2,0:T(8,128)(2,1)}, s32[8,4,8]{2,1,0:T(4,128)S(1)}, bf16[160,128,128]{2,1,0:T(8,128)(2,1)}, ...), condition=%wide.region_5.7_spmd, body=%wide.region_2.6_spmd.sunk | while | flops 205557536 | bytes 12936373 | solution.py:94
  224.7 4.2 %gather_fusion = bf16[32,128,128]{2,1,0:T(8,128)(2,1)} fusion(bf16[160,128,128]{2,1,0:T(8,128)(2,1)} %get-tuple-element.105, s32[1024]{0:T(1024)S(1)} %pad_clamp_fusion.2), kind=kCustom, calls=%fused_computation.1.clone.1 | custom fusion | bytes 2097280 | tf_op jit(solution)/shard_map/while/body/eval_jaxpr/jit(_take)/gather | solution.py:73
  228.9 1.5 copy.45
  231.5 2.0 fusion.86
  236.3 4.2 %gather_fusion = bf16[32,128,128]{2,1,0:T(8,128)(2,1)} fusion(bf16[160,128,128]{2,1,0:T(8,128)(2,1)} %get-tuple-element.105, s32[1024]{0:T(1024)S(1)} %pad_clamp_fusion.2), kind=kCustom, calls=%fused_computation.1.clone.1 | custom fusion | bytes 2097280 | tf_op jit(solution)/shard_map/while/body/eval_jaxpr/jit(_take)/gather | solution.py:73
  240.5 1.5 copy.45
  243.1 2.0 fusion.86
  247.9 4.2 %gather_fusion = bf16[32,128,128]{2,1,0:T(8,128)(2,1)} fusion(bf16[160,128,128]{2,1,0:T(8,128)(2,1)} %get-tuple-element.105, s32[1024]{0:T(1024)S(1)} %pad_clamp_fusion.2), kind=kCustom, calls=%fused_computation.1.clone.1 | custom fusion | bytes 2097280 | tf_op jit(solution)/shard_map/while/body/eval_jaxpr/jit(_take)/gather | solution.py:73
  252.0 1.5 copy.45
  254.6 2.0 fusion.86
  259.4 4.2 %gather_fusion = bf16[32,128,128]{2,1,0:T(8,128)(2,1)} fusion(bf16[160,128,128]{2,1,0:T(8,128)(2,1)} %get-tuple-element.105, s32[1024]{0:T(1024)S(1)} %pad_clamp_fusion.2), kind=kCustom, calls=%fused_computation.1.clone.1 | custom fusion | bytes 2097280 | tf_op jit(solution)/shard_map/while/body/eval_jaxpr/jit(_take)/gather | solution.py:73
  263.6 1.5 copy.45
  266.2 2.0 fusion.86
  271.0 4.2 %gather_fusion = bf16[32,128,128]{2,1,0:T(8,128)(2,1)} fusion(bf16[160,128,128]{2,1,0:T(8,128)(2,1)} %get-tuple-element.105, s32[1024]{0:T(1024)S(1)} %pad_clamp_fusion.2), kind=kCustom, calls=%fused_computation.1.clone.1 | custom fusion | bytes 2097280 | tf_op jit(solution)/shard_map/while/body/eval_jaxpr/jit(_take)/gather | solution.py:73
  275.2 1.5 copy.45
  277.8 2.0 fusion.86
  282.5 4.2 %gather_fusion = bf16[32,128,128]{2,1,0:T(8,128)(2,1)} fusion(bf16[160,128,128]{2,1,0:T(8,128)(2,1)} %get-tuple-element.105, s32[1024]{0:T(1024)S(1)} %pad_clamp_fusion.2), kind=kCustom, calls=%fused_computation.1.clone.1 | custom fusion | bytes 2097280 | tf_op jit(solution)/shard_map/while/body/eval_jaxpr/jit(_take)/gather | solution.py:73
  286.7 1.5 copy.45
  289.3 2.0 fusion.86
  294.1 4.2 %gather_fusion = bf16[32,128,128]{2,1,0:T(8,128)(2,1)} fusion(bf16[160,128,128]{2,1,0:T(8,128)(2,1)} %get-tuple-element.105, s32[1024]{0:T(1024)S(1)} %pad_clamp_fusion.2), kind=kCustom, calls=%fused_computation.1.clone.1 | custom fusion | bytes 2097280 | tf_op jit(solution)/shard_map/while/body/eval_jaxpr/jit(_take)/gather | solution.py:73
  298.3 1.5 copy.45
  300.9 2.0 fusion.86
  305.7 4.2 %gather_fusion = bf16[32,128,128]{2,1,0:T(8,128)(2,1)} fusion(bf16[160,128,128]{2,1,0:T(8,128)(2,1)} %get-tuple-element.105, s32[1024]{0:T(1024)S(1)} %pad_clamp_fusion.2), kind=kCustom, calls=%fused_computation.1.clone.1 | custom fusion | bytes 2097280 | tf_op jit(solution)/shard_map/while/body/eval_jaxpr/jit(_take)/gather | solution.py:73
  309.8 1.5 copy.45
  312.4 2.0 fusion.86
  316.1 1.5 copy.20
  317.7 15.0 %gather_fusion.3 = bf16[4096,64]{1,0:T(8,128)(2,1)} fusion(bf16[4096,64]{1,0:T(8,128)(2,1)S(1)} %bitcast.94, s32[4096]{0:T(1024)S(1)} %get-tuple-element.54), kind=kCustom, calls=%fused_computation.2.clone | custom fusion | bytes 1064960 | tf_op jit(solution)/shard_map/jit(_take)/gather | solution.py:102
  332.7 4.3 %broadcast_select_fusion.1 = bf16[4096,64]{1,0:T(8,128)(2,1)} fusion(bf16[4096,64]{1,0:T(8,128)(2,1)} %gather_fusion.3, pred[4096]{0:T(1024)(128)(4,1)S(1)} %compare_and_fusion.1), kind=kLoop, calls=%fused_computation.65 | loop fusion | flops 262144 | bytes 1052672 | tf_op jit(solution)/shard_map/jit(_take)/select_n | solution.py:102
  337.0 1.5 copy.21
  338.5 16.7 %all_to_all.19 = bf16[16,256,64]{1,2,0:T(8,128)(2,1)S(1)} all-to-all(bf16[16,256,64]{1,2,0:T(8,128)(2,1)S(1)} %copy.21), channel_id=1, replica_groups=mesh['node'=16,'head'=16] {'head'}, dimensions={0} | all-to-all | bytes 1048576 | tf_op jit(solution)/shard_map/all_to_all | solution.py:103
  357.3 7.5 %fusion.32 = bf16[256,1024]{1,0:T(8,128)(2,1)} fusion(f32[256,1024]{1,0:T(8,128)} %copy-done.4, bf16[2048,1024]{1,0:T(8,128)(2,1)} %param.19, bf16[1024,2048]{1,0:T(8,128)(2,1)} %param.18, f32[1024]{0:T(1024)S(1)} %copy-done.14, f32[256]{0:T(256)S(1)} %add_rsqrt_fusion, f32[256]{0:T(256)S(1)} %broadcast_multiply_fusion), kind=kOutput, calls=%fused_computation.47 | convolution fusion | flops 2153775104 | bytes 9967616 | tf_op jit(solution)/shard_map/dot_general | solution.py:111
  (182 shorter events, 45.1 us)
Async XLA Ops:
  6.5 348.7 %copy-start = (bf16[1024,1024]{1,0:T(8,128)(2,1)S(1)}, bf16[1024,1024]{1,0:T(8,128)(2,1)}, u32[]{:S(2)}) copy-start(bf16[1024,1024]{1,0:T(8,128)(2,1)} %param.16) | copy-start | bytes 6291460
  6.5 82.7 %slice-start = ((bf16[1024,1,192]{0,2,1:T(8,128)(2,1)}), bf16[1024,1,64]{0,2,1:T(8,128)(2,1)S(1)}, s32[]{:S(2)}) async-start(bf16[1024,1,192]{0,2,1:T(8,128)(2,1)} %param.15), calls=%async_computation.2 | async-start | bytes 262144 | tf_op jit(solution)/shard_map/slice | solution.py:44
  6.5 82.7 %slice-start.1 = ((bf16[1024,1,192]{0,2,1:T(8,128)(2,1)}), bf16[1024,1,128]{0,2,1:T(8,128)(2,1)S(1)}, s32[]{:S(2)}) async-start(bf16[1024,1,192]{0,2,1:T(8,128)(2,1)} %param.15), calls=%async_computation.3 | async-start | bytes 524288 | tf_op jit(solution)/shard_map/slice | solution.py:44
  6.5 4.9 %copy-start.12 = (s32[1,4096]{1,0:T(1,128)S(1)}, s32[1,4096]{1,0:T(1,128)}, u32[]{:S(2)}) copy-start(s32[1,4096]{1,0:T(1,128)} %param.21) | copy-start | bytes 49156
  6.5 82.7 %all-gather.2.cloned.1.call-start = ((), (), s32[]{:S(2)}) async-start(), calls=%async_computation.1 | async-start | bytes 8912896 | tf_op jit(solution)/shard_map/all_gather | solution.py:47
  95.6 1.1 copy-start.5
  114.4 60.2 %copy-start.13 = (s32[32,8]{0,1:T(8,128)S(1)}, s32[32,8]{0,1:T(8,128)}, u32[]{:S(2)}) copy-start(s32[32,8]{0,1:T(8,128)} %param.20) | copy-start | bytes 3076
  117.8 26.0 %collective-permute-start = (bf16[4096,128]{1,0:T(8,128)(2,1)S(1)}, bf16[4096,128]{1,0:T(8,128)(2,1)S(1)}, u32[]{:S(2)}, u32[]{:S(2)}) collective-permute-start(bf16[4096,128]{1,0:T(8,128)(2,1)S(1)} %broadcast_select_fusion.3), channel_id=1, source_target_pairs={{0,224},{16,240},{32,0},{48,16},{64,32},{80,48},{96,64},{112,80},{... | collective-permute-start | bytes 3145736 | tf_op jit(solution)/shard_map/ppermute | solution.py:16
  143.8 1.0 copy-start.6
  144.8 14.2 %collective-permute-start.1 = (bf16[4096,128]{1,0:T(8,128)(2,1)S(1)}, bf16[4096,128]{1,0:T(8,128)(2,1)S(1)}, u32[]{:S(2)}, u32[]{:S(2)}) collective-permute-start(bf16[4096,128]{1,0:T(8,128)(2,1)S(1)} %collective-permute-done), channel_id=1, source_target_pairs={{0,16},{16,32},{32,48},{48,64},{64,80},{80,96},{96,112},{112,128},... | collective-permute-start | bytes 3145736 | tf_op jit(solution)/shard_map/ppermute | solution.py:16
  159.0 1.0 copy-start.8
  160.0 14.2 %collective-permute-start.2 = (bf16[4096,128]{1,0:T(8,128)(2,1)S(1)}, bf16[4096,128]{1,0:T(8,128)(2,1)S(1)}, u32[]{:S(2)}, u32[]{:S(2)}) collective-permute-start(bf16[4096,128]{1,0:T(8,128)(2,1)S(1)} %collective-permute-done.1), channel_id=1, source_target_pairs={{0,16},{16,32},{32,48},{48,64},{64,80},{80,96},{96,112},{112,128},... | collective-permute-start | bytes 3145736 | tf_op jit(solution)/shard_map/ppermute | solution.py:16
  174.2 20.0 %copy-start.10 = (bf16[4096,128]{1,0:T(8,128)(2,1)}, bf16[4096,128]{1,0:T(8,128)(2,1)S(1)}, u32[]{:S(2)}) copy-start(bf16[4096,128]{1,0:T(8,128)(2,1)S(1)} %collective-permute-done.2) | copy-start | bytes 3145732
  174.2 16.3 %collective-permute-start.3 = (bf16[4096,128]{1,0:T(8,128)(2,1)S(1)}, bf16[4096,128]{1,0:T(8,128)(2,1)}, u32[]{:S(2)}, u32[]{:S(2)}) collective-permute-start(bf16[4096,128]{1,0:T(8,128)(2,1)S(1)} %collective-permute-done.2), channel_id=1, source_target_pairs={{0,16},{16,32},{32,48},{48,64},{64,80},{80,96},{96,112},{112,128},... | collective-permute-start | bytes 3145736 | tf_op jit(solution)/shard_map/ppermute | solution.py:16
  190.5 26.6 %collective-permute-start.4 = (bf16[4096,128]{1,0:T(8,128)(2,1)}, bf16[4096,128]{1,0:T(8,128)(2,1)}, u32[]{:S(2)}, u32[]{:S(2)}) collective-permute-start(bf16[4096,128]{1,0:T(8,128)(2,1)} %collective-permute-done.3), channel_id=1, source_target_pairs={{0,16},{16,32},{32,48},{48,64},{64,80},{80,96},{96,112},{112,128},... | collective-permute-start | bytes 3145736 | tf_op jit(solution)/shard_map/ppermute | solution.py:16
  217.1 2.9 copy-start.11
  218.5 1.6 copy-start.9
  220.0 1.3 copy-start.7
  221.4 2.3 copy-start.3
  231.5 2.0 copy-start.1
  243.1 2.0 copy-start.1
  254.6 2.0 copy-start.1
  266.2 2.0 copy-start.1
  277.8 2.0 copy-start.1
  289.3 2.0 copy-start.1
  300.9 2.0 copy-start.1
  312.4 2.0 copy-start.1
  332.7 22.6 %copy-start.2 = (bf16[256,1024]{1,0:T(8,128)(2,1)S(1)}, bf16[256,1024]{1,0:T(8,128)(2,1)}, u32[]{:S(2)}) copy-start(bf16[256,1024]{1,0:T(8,128)(2,1)} %param.13) | copy-start | bytes 1572868
  355.2 2.1 copy-start.14
  356.1 1.0 copy-start.4
Sparse Core Ops, SparseCore 0:
  11.6 77.6 all-gather.1
where the time goes:
time: 373 us; the launch traced here: 372 us
  local copies, waits for them, and re-layouts  141 us (38%)
  waiting for transfers between devices  132 us (35%)
  matrix products  38.1 us (10%)
  other arithmetic  25.3 us (7%)
  blocking collectives  16.7 us (4%)
  between operations  13.6 us (4%)
  starting transfers between devices  4.69 us (1%)
    all_gather x1, waiting for transfers between devices, shards(): lax.all_gather(normed, 'head', axis=0, tiled=True)  77.8 us
    ppermute x5, waiting for transfers between devices, passed_along(): return lax.ppermute(x, axis, [(i, (i + by) % size) for i in range(size)])  53.9 us
    gather x16, local copies, waits for them, and re-layouts, attend(): picked = jnp.take(window_tiles, columns.reshape(tile_group * NNZ), axis=0)  45.3 us
    all_to_all x1, blocking collectives, shards(): lax.all_to_all(restored, 'head', split_axis=0, concat_axis=1, tiled=True)  16.7 us
    sub x8, matrix products, attend(): expd = jnp.exp(scores - row_max)  15.7 us
    scatter x1, local copies, waits for them, and re-layouts, shards(): inverse_order = jnp.zeros((rows_part,), jnp.int32).at[partition_permutati...  15.7 us
    gather x1, local copies, waits for them, and re-layouts, shards(): keyval = jnp.take(keyval_rows, partition_permutation, axis=0)  15 us
    gather x1, local copies, waits for them, and re-layouts, shards(): restored = jnp.take(attended, inverse_order, axis=0)  15 us
  transfers between devices with their start and end apart: 6, of which 4 were waited for; matrix products, arithmetic and copies ran while one was open for 10% of the time, Pallas kernels for 0%

commit v1 on v0

--- a/solution.py
+++ b/solution.py
@@ -100,7 +100,10 @@
         .set(jnp.arange(rows_part, dtype=jnp.int32))
     )
     restored = jnp.take(attended, inverse_order, axis=0)
-    gathered_heads = lax.all_to_all(restored, "head", split_axis=0, concat_axis=1, tiled=True)
+    count = lax.axis_size("head")
+    pieces = jnp.stack(jnp.split(restored, count, axis=0), axis=0)
+    pieces = lax.all_to_all(pieces, "head", split_axis=0, concat_axis=0)
+    gathered_heads = jnp.concatenate(pieces, axis=1)
     residual = features.astype(jnp.float32) + jnp.dot(
         gathered_heads, out_weight, preferred_element_type=jnp.float32
     )

time: 373 us -> 383 us (1.027)
  local copies, waits for them, and re-layouts: 141 us -> 151 us
    unnamed x32 -> x47, local copies, waits for them, and re-layouts: 10.4 us -> 19.9 us
where the time goes in v1:
time: 383 us; the launch traced here: 381 us
  local copies, waits for them, and re-layouts  151 us (39%)
  waiting for transfers between devices  132 us (34%)
  matrix products  38.1 us (10%)
  other arithmetic  24.4 us (6%)
  blocking collectives  16.7 us (4%)
  between operations  13.7 us (4%)
  starting transfers between devices  4.69 us (1%)
    all_gather x1, waiting for transfers between devices, shards(): lax.all_gather(normed, 'head', axis=0, tiled=True)  77.8 us
    ppermute x5, waiting for transfers between devices, passed_along(): return lax.ppermute(x, axis, [(i, (i + by) % size) for i in range(size)])  53.9 us
    gather x16, local copies, waits for them, and re-layouts, attend(): picked = jnp.take(window_tiles, columns.reshape(tile_group * NNZ), axis=0)  45.3 us
    unnamed x47, local copies, waits for them, and re-layouts  19.9 us
    all_to_all x1, blocking collectives, shards(): pieces = lax.all_to_all(pieces, 'head', split_axis=0, concat_axis=0)  16.7 us
    sub x8, matrix products, attend(): expd = jnp.exp(scores - row_max)  15.7 us
    scatter x1, local copies, waits for them, and re-layouts, shards(): inverse_order = jnp.zeros((rows_part,), jnp.int32).at[partition_permutati...  15.7 us
    gather x1, local copies, waits for them, and re-layouts, shards(): keyval = jnp.take(keyval_rows, partition_permutation, axis=0)  15 us
  transfers between devices with their start and end apart: 6, of which 4 were waited for; matrix products, arithmetic and copies ran while one was open for 10% of the time, Pallas kernels for 0%

profile of v1, /device:TPU:96, one launch (start us, length us, event | category | flops | bytes accessed | tf_op | source)
XLA Modules:
  0.0 380.8 jit_solution(12906450693837003388)
XLA Ops:
  9.3 2.1 fusion.37
  11.5 77.8 %all-gather.2.cloned.1.call-done = bf16[4096,1024]{1,0:T(8,128)(2,1)} async-done(((bf16[256,1024]{1,0:T(8,128)(2,1)}), bf16[4096,1024]{1,0:T(8,128)(2,1)}) %all-gather.2.cloned.1.call-update) | async-done | bytes 8388624 | tf_op jit(solution)/shard_map/all_gather | solution.py:47
  89.3 6.3 %fusion.23 = bf16[4096,1,192]{0,2,1:T(8,128)(2,1)S(1)} fusion(bf16[4096,1024]{1,0:T(8,128)(2,1)} %all-gather.2.cloned.1.call-done, bf16[1024,1,64]{0,2,1:T(8,128)(2,1)S(1)} %slice-done, bf16[1024,1,128]{0,2,1:T(8,128)(2,1)S(1)} %slice-done.1), kind=kOutput, calls=%fused_computation.33 | convolution fusion | flops 1612185600 | bytes 10354688 | tf_op jit(solution)/shard_map/dot_general | solution.py:46
  97.8 1.6 copy.26
  99.4 15.0 %gather_fusion.1 = bf16[4096,128]{1,0:T(8,128)(2,1)} fusion(bf16[4096,128]{1,0:T(8,128)(2,1)S(1)} %copy.26, s32[4096]{0:T(1024)S(1)} %broadcast_clamp_fusion), kind=kCustom, calls=%fused_computation.3 | custom fusion | bytes 2113536 | tf_op jit(solution)/shard_map/jit(_take)/gather | solution.py:55
  114.4 3.4 broadcast_select_fusion.3
  118.3 25.5 %collective-permute-done = bf16[4096,128]{1,0:T(8,128)(2,1)S(1)} collective-permute-done((bf16[4096,128]{1,0:T(8,128)(2,1)S(1)}, bf16[4096,128]{1,0:T(8,128)(2,1)S(1)}, u32[]{:S(2)}, u32[]{:S(2)}) %collective-permute-start) | collective-permute-done | bytes 1048608 | tf_op jit(solution)/shard_map/ppermute | solution.py:16
  144.8 14.2 %collective-permute-done.1 = bf16[4096,128]{1,0:T(8,128)(2,1)S(1)} collective-permute-done((bf16[4096,128]{1,0:T(8,128)(2,1)S(1)}, bf16[4096,128]{1,0:T(8,128)(2,1)S(1)}, u32[]{:S(2)}, u32[]{:S(2)}) %collective-permute-start.1) | collective-permute-done | bytes 1048608 | tf_op jit(solution)/shard_map/ppermute | solution.py:16
  160.0 14.2 %collective-permute-done.2 = bf16[4096,128]{1,0:T(8,128)(2,1)S(1)} collective-permute-done((bf16[4096,128]{1,0:T(8,128)(2,1)S(1)}, bf16[4096,128]{1,0:T(8,128)(2,1)S(1)}, u32[]{:S(2)}, u32[]{:S(2)}) %collective-permute-start.2) | collective-permute-done | bytes 1048608 | tf_op jit(solution)/shard_map/ppermute | solution.py:16
  174.7 15.7 %scatter_custom_fusion = s32[4096]{0:T(1024)S(1)} fusion(s32[4096]{0:T(1024)S(1)} %bitcast.165, s32[4096]{0:T(1024)S(1)} %iota.3, s32[]{:T(128)} %copy.84), kind=kCustom, calls=%fused_computation.116 | custom fusion | bytes 16388 | tf_op jit(solution)/shard_map/scatter | solution.py:100
  190.5 3.7 collective-permute-start.4
  194.2 1.9 slice_bitcast_fusion.15
  196.1 1.5 copy.27
  197.6 15.0 %gather_fusion.2 = bf16[4096,64]{1,0:T(8,128)(2,1)} fusion(bf16[4096,64]{1,0:T(8,128)(2,1)S(1)} %copy.27, s32[4096]{0:T(1024)S(1)} %get-tuple-element.58), kind=kCustom, calls=%fused_computation.clone | custom fusion | bytes 1064960 | tf_op jit(solution)/shard_map/jit(_take)/gather | solution.py:56
  212.6 3.4 broadcast_select_fusion.2
  218.5 1.4 bitcast_dynamic-update-slice_fusion.3
  221.4 2.3 copy-done.3
  223.7 92.5 %while.10 = (s32[]{:T(128)}, bf16[8,512,64]{1,2,0:T(8,128)(2,1)}, s32[8,4,8]{2,1,0:T(4,128)S(1)}, bf16[160,128,128]{2,1,0:T(8,128)(2,1)}, bf16[8,512,64]{1,2,0:T(8,128)(2,1)}, /*index=5*/s32[]{:T(128)}) while((s32[]{:T(128)}, bf16[8,512,64]{1,2,0:T(8,128)(2,1)}, s32[8,4,8]{2,1,0:T(4,128)S(1)}, bf16[160,128,128]{2,1,0:T(8,128)(2,1)}, ...), condition=%wide.region_5.7_spmd, body=%wide.region_2.6_spmd.sunk | while | flops 205557536 | bytes 12936373 | solution.py:94
  224.7 4.2 %gather_fusion = bf16[32,128,128]{2,1,0:T(8,128)(2,1)} fusion(bf16[160,128,128]{2,1,0:T(8,128)(2,1)} %get-tuple-element.110, s32[1024]{0:T(1024)S(1)} %pad_clamp_fusion.2), kind=kCustom, calls=%fused_computation.1.clone.1 | custom fusion | bytes 2097280 | tf_op jit(solution)/shard_map/while/body/eval_jaxpr/jit(_take)/gather | solution.py:73
  228.9 1.5 copy.54
  231.5 2.0 fusion.102
  236.3 4.2 %gather_fusion = bf16[32,128,128]{2,1,0:T(8,128)(2,1)} fusion(bf16[160,128,128]{2,1,0:T(8,128)(2,1)} %get-tuple-element.110, s32[1024]{0:T(1024)S(1)} %pad_clamp_fusion.2), kind=kCustom, calls=%fused_computation.1.clone.1 | custom fusion | bytes 2097280 | tf_op jit(solution)/shard_map/while/body/eval_jaxpr/jit(_take)/gather | solution.py:73
  240.5 1.5 copy.54
  243.1 2.0 fusion.102
  247.9 4.2 %gather_fusion = bf16[32,128,128]{2,1,0:T(8,128)(2,1)} fusion(bf16[160,128,128]{2,1,0:T(8,128)(2,1)} %get-tuple-element.110, s32[1024]{0:T(1024)S(1)} %pad_clamp_fusion.2), kind=kCustom, calls=%fused_computation.1.clone.1 | custom fusion | bytes 2097280 | tf_op jit(solution)/shard_map/while/body/eval_jaxpr/jit(_take)/gather | solution.py:73
  252.0 1.5 copy.54
  254.6 2.0 fusion.102
  259.4 4.2 %gather_fusion = bf16[32,128,128]{2,1,0:T(8,128)(2,1)} fusion(bf16[160,128,128]{2,1,0:T(8,128)(2,1)} %get-tuple-element.110, s32[1024]{0:T(1024)S(1)} %pad_clamp_fusion.2), kind=kCustom, calls=%fused_computation.1.clone.1 | custom fusion | bytes 2097280 | tf_op jit(solution)/shard_map/while/body/eval_jaxpr/jit(_take)/gather | solution.py:73
  263.6 1.5 copy.54
  266.2 2.0 fusion.102
  271.0 4.2 %gather_fusion = bf16[32,128,128]{2,1,0:T(8,128)(2,1)} fusion(bf16[160,128,128]{2,1,0:T(8,128)(2,1)} %get-tuple-element.110, s32[1024]{0:T(1024)S(1)} %pad_clamp_fusion.2), kind=kCustom, calls=%fused_computation.1.clone.1 | custom fusion | bytes 2097280 | tf_op jit(solution)/shard_map/while/body/eval_jaxpr/jit(_take)/gather | solution.py:73
  275.2 1.5 copy.54
  277.8 2.0 fusion.102
  282.5 4.2 %gather_fusion = bf16[32,128,128]{2,1,0:T(8,128)(2,1)} fusion(bf16[160,128,128]{2,1,0:T(8,128)(2,1)} %get-tuple-element.110, s32[1024]{0:T(1024)S(1)} %pad_clamp_fusion.2), kind=kCustom, calls=%fused_computation.1.clone.1 | custom fusion | bytes 2097280 | tf_op jit(solution)/shard_map/while/body/eval_jaxpr/jit(_take)/gather | solution.py:73
  286.7 1.5 copy.54
  289.3 2.0 fusion.102
  294.1 4.2 %gather_fusion = bf16[32,128,128]{2,1,0:T(8,128)(2,1)} fusion(bf16[160,128,128]{2,1,0:T(8,128)(2,1)} %get-tuple-element.110, s32[1024]{0:T(1024)S(1)} %pad_clamp_fusion.2), kind=kCustom, calls=%fused_computation.1.clone.1 | custom fusion | bytes 2097280 | tf_op jit(solution)/shard_map/while/body/eval_jaxpr/jit(_take)/gather | solution.py:73
  298.3 1.5 copy.54
  300.9 2.0 fusion.102
  305.7 4.2 %gather_fusion = bf16[32,128,128]{2,1,0:T(8,128)(2,1)} fusion(bf16[160,128,128]{2,1,0:T(8,128)(2,1)} %get-tuple-element.110, s32[1024]{0:T(1024)S(1)} %pad_clamp_fusion.2), kind=kCustom, calls=%fused_computation.1.clone.1 | custom fusion | bytes 2097280 | tf_op jit(solution)/shard_map/while/body/eval_jaxpr/jit(_take)/gather | solution.py:73
  309.8 1.5 copy.54
  312.4 2.0 fusion.102
  316.1 1.5 copy.29
  317.7 15.0 %gather_fusion.3 = bf16[4096,64]{1,0:T(8,128)(2,1)} fusion(bf16[4096,64]{1,0:T(8,128)(2,1)S(1)} %bitcast.157, s32[4096]{0:T(1024)S(1)} %get-tuple-element.59), kind=kCustom, calls=%fused_computation.2.clone | custom fusion | bytes 1064960 | tf_op jit(solution)/shard_map/jit(_take)/gather | solution.py:102
  332.7 3.4 broadcast_select_fusion.1
  346.2 1.5 copy.30
  347.7 16.7 %all_to_all.5 = bf16[16,256,64]{1,2,0:T(8,128)(2,1)S(1)} all-to-all(bf16[16,256,64]{1,2,0:T(8,128)(2,1)S(1)} %copy.30), channel_id=1, replica_groups=mesh['node'=16,'head'=16] {'head'}, dimensions={0} | all-to-all | bytes 1048576 | tf_op jit(solution)/shard_map/all_to_all | solution.py:105
  366.5 7.5 %fusion.32 = bf16[256,1024]{1,0:T(8,128)(2,1)} fusion(f32[256,1024]{1,0:T(8,128)} %copy-done.4, bf16[2048,1024]{1,0:T(8,128)(2,1)} %param.19, bf16[1024,2048]{1,0:T(8,128)(2,1)} %param.18, f32[1024]{0:T(1024)S(1)} %copy-done.14, f32[256]{0:T(256)S(1)} %add_rsqrt_fusion, f32[256]{0:T(256)S(1)} %broadcast_multiply_fusion), kind=kOutput, calls=%fused_computation.47 | convolution fusion | flops 2153775104 | bytes 9967616 | tf_op jit(solution)/shard_map/dot_general | solution.py:114
  (198 shorter events, 55.2 us)
Async XLA Ops:
  6.5 357.9 %copy-start = (bf16[1024,1024]{1,0:T(8,128)(2,1)S(1)}, bf16[1024,1024]{1,0:T(8,128)(2,1)}, u32[]{:S(2)}) copy-start(bf16[1024,1024]{1,0:T(8,128)(2,1)} %param.16) | copy-start | bytes 6291460
  6.5 82.7 %slice-start = ((bf16[1024,1,192]{0,2,1:T(8,128)(2,1)}), bf16[1024,1,64]{0,2,1:T(8,128)(2,1)S(1)}, s32[]{:S(2)}) async-start(bf16[1024,1,192]{0,2,1:T(8,128)(2,1)} %param.15), calls=%async_computation.2 | async-start | bytes 262144 | tf_op jit(solution)/shard_map/slice | solution.py:44
  6.5 82.7 %slice-start.1 = ((bf16[1024,1,192]{0,2,1:T(8,128)(2,1)}), bf16[1024,1,128]{0,2,1:T(8,128)(2,1)S(1)}, s32[]{:S(2)}) async-start(bf16[1024,1,192]{0,2,1:T(8,128)(2,1)} %param.15), calls=%async_computation.3 | async-start | bytes 524288 | tf_op jit(solution)/shard_map/slice | solution.py:44
  6.5 4.9 %copy-start.12 = (s32[1,4096]{1,0:T(1,128)S(1)}, s32[1,4096]{1,0:T(1,128)}, u32[]{:S(2)}) copy-start(s32[1,4096]{1,0:T(1,128)} %param.21) | copy-start | bytes 49156
  6.5 82.7 %all-gather.2.cloned.1.call-start = ((), (), s32[]{:S(2)}) async-start(), calls=%async_computation.1 | async-start | bytes 8912896 | tf_op jit(solution)/shard_map/all_gather | solution.py:47
  95.6 1.1 copy-start.5
  114.4 60.2 %copy-start.13 = (s32[32,8]{0,1:T(8,128)S(1)}, s32[32,8]{0,1:T(8,128)}, u32[]{:S(2)}) copy-start(s32[32,8]{0,1:T(8,128)} %param.20) | copy-start | bytes 3076
  117.8 26.0 %collective-permute-start = (bf16[4096,128]{1,0:T(8,128)(2,1)S(1)}, bf16[4096,128]{1,0:T(8,128)(2,1)S(1)}, u32[]{:S(2)}, u32[]{:S(2)}) collective-permute-start(bf16[4096,128]{1,0:T(8,128)(2,1)S(1)} %broadcast_select_fusion.3), channel_id=1, source_target_pairs={{0,224},{16,240},{32,0},{48,16},{64,32},{80,48},{96,64},{112,80},{... | collective-permute-start | bytes 3145736 | tf_op jit(solution)/shard_map/ppermute | solution.py:16
  143.8 1.0 copy-start.6
  144.8 14.2 %collective-permute-start.1 = (bf16[4096,128]{1,0:T(8,128)(2,1)S(1)}, bf16[4096,128]{1,0:T(8,128)(2,1)S(1)}, u32[]{:S(2)}, u32[]{:S(2)}) collective-permute-start(bf16[4096,128]{1,0:T(8,128)(2,1)S(1)} %collective-permute-done), channel_id=1, source_target_pairs={{0,16},{16,32},{32,48},{48,64},{64,80},{80,96},{96,112},{112,128},... | collective-permute-start | bytes 3145736 | tf_op jit(solution)/shard_map/ppermute | solution.py:16
  159.0 1.0 copy-start.8
  160.0 14.2 %collective-permute-start.2 = (bf16[4096,128]{1,0:T(8,128)(2,1)S(1)}, bf16[4096,128]{1,0:T(8,128)(2,1)S(1)}, u32[]{:S(2)}, u32[]{:S(2)}) collective-permute-start(bf16[4096,128]{1,0:T(8,128)(2,1)S(1)} %collective-permute-done.1), channel_id=1, source_target_pairs={{0,16},{16,32},{32,48},{48,64},{64,80},{80,96},{96,112},{112,128},... | collective-permute-start | bytes 3145736 | tf_op jit(solution)/shard_map/ppermute | solution.py:16
  174.2 20.0 %copy-start.10 = (bf16[4096,128]{1,0:T(8,128)(2,1)}, bf16[4096,128]{1,0:T(8,128)(2,1)S(1)}, u32[]{:S(2)}) copy-start(bf16[4096,128]{1,0:T(8,128)(2,1)S(1)} %collective-permute-done.2) | copy-start | bytes 3145732
  174.2 16.3 %collective-permute-start.3 = (bf16[4096,128]{1,0:T(8,128)(2,1)S(1)}, bf16[4096,128]{1,0:T(8,128)(2,1)}, u32[]{:S(2)}, u32[]{:S(2)}) collective-permute-start(bf16[4096,128]{1,0:T(8,128)(2,1)S(1)} %collective-permute-done.2), channel_id=1, source_target_pairs={{0,16},{16,32},{32,48},{48,64},{64,80},{80,96},{96,112},{112,128},... | collective-permute-start | bytes 3145736 | tf_op jit(solution)/shard_map/ppermute | solution.py:16
  190.5 26.6 %collective-permute-start.4 = (bf16[4096,128]{1,0:T(8,128)(2,1)}, bf16[4096,128]{1,0:T(8,128)(2,1)}, u32[]{:S(2)}, u32[]{:S(2)}) collective-permute-start(bf16[4096,128]{1,0:T(8,128)(2,1)} %collective-permute-done.3), channel_id=1, source_target_pairs={{0,16},{16,32},{32,48},{48,64},{64,80},{80,96},{96,112},{112,128},... | collective-permute-start | bytes 3145736 | tf_op jit(solution)/shard_map/ppermute | solution.py:16
  217.1 2.9 copy-start.11
  218.5 1.6 copy-start.9
  220.0 1.3 copy-start.7
  221.4 2.3 copy-start.3
  231.5 2.0 copy-start.1
  243.1 2.0 copy-start.1
  254.6 2.0 copy-start.1
  266.2 2.0 copy-start.1
  277.8 2.0 copy-start.1
  289.3 2.0 copy-start.1
  300.9 2.0 copy-start.1
  312.4 2.0 copy-start.1
  338.6 25.9 %copy-start.2 = (bf16[256,1024]{1,0:T(8,128)(2,1)S(1)}, bf16[256,1024]{1,0:T(8,128)(2,1)}, u32[]{:S(2)}) copy-start(bf16[256,1024]{1,0:T(8,128)(2,1)} %param.13) | copy-start | bytes 1572868
  364.5 2.1 copy-start.14
  365.3 1.0 copy-start.4
Sparse Core Ops, SparseCore 0:
  11.6 77.6 all-gather.1
